TPU v7x, 32 devices: a whole 2x2x4 slice. The times are simulated.
32 devices in a mesh: sta: 8 (over y, x, core), win: 4 (over z).
Axes of the slice: x: 2, y: 2, z: 4, core: 2. Of those that a mesh axis runs over, the one named last changes fastest.
Arguments:
- green: bfloat16 [8, 3, 2, 256, 2048], P('sta', None, None, None, 'win'), may hold values from -0.0390625 to 0.0390625
- records: float32 [8, 3, 2, 2048], P('sta', None, None, 'win'), may hold values from -6 to 6
- onsets: int32 [256, 32], P('sta', 'win'), may hold values from 0 to 4095
- mask: int32 [8, 3], P('sta'), may hold values 0 or 1
Outputs:
- slip: float32 [256, 32], P('sta', 'win')
- direction: float32 [256, 32], P('sta', 'win')
- misfit: float32 [8, 3, 2, 2048], P('sta', None, None, 'win')
All inputs are finite; a program needn't handle non-finite values. No bound on the sum of `mask` on one device may be relied on, other than what follows from the above.
Results may differ from a plain program's by a relative error of at most 0.007.
Values may be sent and summed in bfloat16 or wider, within the bound.
A program may use at most 64 MiB of HBM per device.

v0:
```python
import math

import jax
import jax.numpy as jnp
from jax import lax
from jax.sharding import PartitionSpec as P

SAMPLES = 4096
ITERS = 2


TWO_PI = 2.0 * math.pi


def phase_tables(onset_block, frequency):
    turns = onset_block[:, :, None] * frequency[None, None, :] % SAMPLES
    angle = turns.astype(jnp.float32) * (TWO_PI / SAMPLES)
    return (jnp.cos(angle), jnp.sin(angle))


def spectra_from(values, cosine, sine):
    real_part = jnp.sum(values[:, :, None] * cosine, axis=1)
    imag_part = -jnp.sum(values[:, :, None] * sine, axis=1)
    return jnp.concatenate([real_part, imag_part], axis=1).astype(jnp.bfloat16)


def project_with(combined, cosine, sine):
    bins = cosine.shape[2]
    comb_re = combined[:, :bins]
    comb_im = combined[:, bins:]
    return jnp.sum(cosine * comb_re[:, None, :] - sine * comb_im[:, None, :], axis=2)


def contract(green_part, spectrum):
    bins = green_part.shape[4]
    spec_re = spectrum[:, :bins].astype(jnp.float32)
    spec_im = spectrum[:, bins:].astype(jnp.float32)
    green_re = green_part[:, :, 0].astype(jnp.float32)
    green_im = green_part[:, :, 1].astype(jnp.float32)
    real_part = jnp.sum(green_re * spec_re - green_im * spec_im, axis=2)
    imag_part = jnp.sum(green_re * spec_im + green_im * spec_re, axis=2)
    return jnp.stack([real_part, imag_part], axis=2)


def back_project(green_part, rounded):
    green_re = green_part[:, :, 0].astype(jnp.float32)
    green_im = green_part[:, :, 1].astype(jnp.float32)
    trace_re = rounded[:, :, 0].astype(jnp.float32)[:, :, None, :]
    trace_im = rounded[:, :, 1].astype(jnp.float32)[:, :, None, :]
    part_re = jnp.sum(green_re * trace_re + green_im * trace_im, axis=(0, 1))
    part_im = jnp.sum(green_re * trace_im - green_im * trace_re, axis=(0, 1))
    return jnp.concatenate([part_re, part_im], axis=1)


def local(green, records, onsets, mask):
    slab_bins = green.shape[4]
    frequency = jnp.arange(slab_bins, dtype=jnp.int32) + lax.axis_index("win") * slab_bins
    weight = mask.astype(jnp.float32)[:, :, None, None]
    patch_rows = onsets.shape[0]
    all_patches = patch_rows * lax.axis_size("sta")
    all_windows = onsets.shape[1] * lax.axis_size("win")
    onset_rows = lax.all_gather(onsets, "win", axis=1, tiled=True)
    cosine, sine = phase_tables(onset_rows, frequency)

    def apply_adjoint(left):
        rounded = (left * weight).astype(jnp.bfloat16)
        combined = lax.psum_scatter(
            back_project(green, rounded), "sta", scatter_dimension=0, tiled=True
        )
        rows = project_with(combined, cosine, sine)
        return lax.psum_scatter(rows, "win", scatter_dimension=1, tiled=True)

    def data_size(left):
        return jnp.sqrt(lax.psum(jnp.sum(left * left), ("sta", "win")))

    def model_size(right):
        return jnp.sqrt(lax.psum(jnp.sum(right * right), ("sta", "win")))

    left = records * weight
    beta_norm = data_size(left)
    left = left / beta_norm
    right = apply_adjoint(left)
    alpha_norm = model_size(right)
    right = right / alpha_norm
    search = right
    estimate = jnp.zeros(onsets.shape, jnp.float32)
    phi_bar = beta_norm
    rho_bar = alpha_norm
    for sweep in range(ITERS):
        apply_rows = lax.all_gather(right, "win", axis=1, tiled=True)
        spectrum = spectra_from(apply_rows, cosine, sine)
        data = contract(green, lax.all_gather(spectrum, "sta", axis=0, tiled=True))
        left = data * weight - alpha_norm * left
        beta_norm = data_size(left)
        left = left / beta_norm
        right = apply_adjoint(left) - beta_norm * right
        alpha_norm = model_size(right)
        right = right / alpha_norm
        rho_value = jnp.sqrt(rho_bar * rho_bar + beta_norm * beta_norm)
        cosine_rot = rho_bar / rho_value
        sine_rot = beta_norm / rho_value
        theta_rot = sine_rot * alpha_norm
        rho_bar = -cosine_rot * alpha_norm
        phi_step = cosine_rot * phi_bar
        phi_bar = sine_rot * phi_bar
        estimate = estimate + phi_step / rho_value * search
        search = right - theta_rot / rho_value * search
    return (estimate, search * math.sqrt(all_patches * all_windows), phi_bar * left)


def solution(mesh):
    return jax.shard_map(
        local,
        mesh=mesh,
        in_specs=(
            P("sta", None, None, None, "win"),
            P("sta", None, None, "win"),
            P("sta", "win"),
            P("sta", None),
        ),
        out_specs=(P("sta", "win"), P("sta", "win"), P("sta", None, None, "win")),
        check_vma=False,
    )
```

profile of v0, /device:TPU:0, one launch (start us, length us, event | category | flops | bytes accessed | tf_op | source)
XLA Modules:
  0.0 530.2 jit_solution(13713221137934037425)
XLA Ops:
  7.9 1.4 multiply_reduce_fusion.6
  9.3 42.2 %psum.42 = f32[]{:T(128)} all-reduce(f32[]{:T(128)} %multiply_reduce_fusion.6), channel_id=1, replica_groups=mesh['sta'=8,'win'=4] {'sta','win'}, use_global_device_ids=true, to_apply=%region_1.2 | all-reduce | flops 1 | bytes 8 | tf_op jit(solution)/shard_map/psum | solution.py:74
  52.1 0.8 multiply_convert_fusion.2
  52.9 2.0 fusion.4
  55.0 1.1 pad_maximum_fusion
  56.1 13.2 %all_gather.15 = s32[32,32]{0,1:T(8,128)S(1)} all-gather(s32[32,8]{0,1:T(8,128)S(1)} %copy-done.2), channel_id=1, replica_groups=mesh['sta'=8,'win'=4] {'win'}, dimensions={1}, use_global_device_ids=true | all-gather | bytes 5120 | tf_op jit(solution)/shard_map/all_gather | solution.py:62
  70.7 21.5 %reduce-scatter.4.cloned.1.call-done = f32[32,1024]{1,0:T(8,128)} async-done(((f32[256,1024]{1,0:T(8,128)}), f32[32,1024]{1,0:T(8,128)}) %reduce-scatter.4.cloned.1.call-update) | async-done | bytes 131088 | tf_op jit(solution)/shard_map/reduce_scatter | solution.py:67
  92.2 0.9 fusion.38
  93.1 9.7 %subtract_reduce_fusion.2 = f32[32,32]{1,0:T(8,128)S(1)} fusion(f32[32,512]{1,0:T(8,128)S(1)} %get-tuple-element.39, f32[32,512]{1,0:T(8,128)S(1)} %get-tuple-element.38, s32[512]{0:T(512)S(1)} %iota_add_fusion, s32[32,32]{1,0:T(8,128)S(1)} %copy.23), kind=kLoop, calls=%fused_computation.34 | loop fusion | flops 9436160 | bytes 141312 | tf_op jit(solution)/shard_map/reduce_sum | solution.py:31
  102.8 18.7 %all-reduce = f32[32,32]{0,1:T(8,128)S(1)} all-reduce(f32[32,32]{0,1:T(8,128)S(1)} %copy.26), channel_id=3, replica_groups=mesh['sta'=8,'win'=4] {'win'}, use_global_device_ids=true, to_apply=%region_6.7.clone | all-reduce | flops 1024 | bytes 8192
  122.1 37.0 %psum.43 = f32[]{:T(128)} all-reduce(f32[]{:T(128)} %multiply_reduce_fusion.9), channel_id=1, replica_groups=mesh['sta'=8,'win'=4] {'sta','win'}, use_global_device_ids=true, to_apply=%region_8.9 | all-reduce | flops 1 | bytes 8 | tf_op jit(solution)/shard_map/psum | solution.py:77
  159.9 13.8 %all_gather.16 = f32[32,32]{0,1:T(8,128)S(1)} all-gather(f32[32,8]{0,1:T(8,128)S(1)} %dynamic-slice_divide_fusion), channel_id=1, replica_groups=mesh['sta'=8,'win'=4] {'win'}, dimensions={1}, use_global_device_ids=true | all-gather | bytes 5120 | tf_op jit(solution)/shard_map/all_gather | solution.py:90
  173.7 9.4 %multiply_reduce_fusion.3 = (bf16[32,512]{1,0:T(8,128)(2,1)S(1)}, f32[32,512]{1,0:T(8,128)S(1)}) fusion(f32[32,32]{1,0:T(8,128)S(1)} %copy.27, s32[512]{0:T(512)S(1)} %iota_add_fusion, s32[32,32]{1,0:T(8,128)S(1)} %copy.23), kind=kLoop, calls=%fused_computation.33 | loop fusion | flops 9404416 | bytes 108544 | tf_op jit(solution)/shard_map/reduce_sum | solution.py:22
  183.2 10.9 %all_gather.17 = bf16[256,1024]{1,0:T(8,128)(2,1)S(1)} all-gather(bf16[32,1024]{1,0:T(8,128)(2,1)S(1)} %pad_maximum_fusion.3), channel_id=1, replica_groups=mesh['sta'=8,'win'=4] {'sta'}, dimensions={0}, use_global_device_ids=true | all-gather | bytes 589824 | tf_op jit(solution)/shard_map/all_gather | solution.py:92
  195.6 38.4 %psum.44 = f32[]{:T(128)} all-reduce(f32[]{:T(128)} %get-tuple-element.28), channel_id=1, replica_groups=mesh['sta'=8,'win'=4] {'sta','win'}, use_global_device_ids=true, to_apply=%region_14.15 | all-reduce | flops 1 | bytes 8 | tf_op jit(solution)/shard_map/psum | solution.py:74
  235.3 1.1 pad_maximum_fusion.1
  236.6 36.9 %reduce-scatter.6.cloned.1.call-done = f32[32,1024]{1,0:T(8,128)} async-done(((f32[256,1024]{1,0:T(8,128)}), f32[32,1024]{1,0:T(8,128)}) %reduce-scatter.6.cloned.1.call-update) | async-done | bytes 131088 | tf_op jit(solution)/shard_map/reduce_scatter | solution.py:67
  273.5 0.9 fusion.37
  274.4 9.7 %subtract_reduce_fusion.1 = f32[32,32]{1,0:T(8,128)S(1)} fusion(f32[32,512]{1,0:T(8,128)S(1)} %get-tuple-element.37, f32[32,512]{1,0:T(8,128)S(1)} %get-tuple-element.36, s32[512]{0:T(512)S(1)} %iota_add_fusion, s32[32,32]{1,0:T(8,128)S(1)} %copy.23), kind=kLoop, calls=%fused_computation.31 | loop fusion | flops 9436160 | bytes 141312 | tf_op jit(solution)/shard_map/reduce_sum | solution.py:31
  284.1 18.7 %all-reduce.1 = f32[32,32]{0,1:T(8,128)S(1)} all-reduce(f32[32,32]{0,1:T(8,128)S(1)} %copy.28), channel_id=5, replica_groups=mesh['sta'=8,'win'=4] {'win'}, use_global_device_ids=true, to_apply=%region_19.20.clone | all-reduce | flops 1024 | bytes 8192
  303.4 37.0 %psum.45 = f32[]{:T(128)} all-reduce(f32[]{:T(128)} %multiply_reduce_fusion.8), channel_id=1, replica_groups=mesh['sta'=8,'win'=4] {'sta','win'}, use_global_device_ids=true, to_apply=%region_21.22 | all-reduce | flops 1 | bytes 8 | tf_op jit(solution)/shard_map/psum | solution.py:77
  341.1 13.8 %all_gather.18 = f32[32,32]{0,1:T(8,128)S(1)} all-gather(f32[32,8]{0,1:T(8,128)S(1)} %broadcast_divide_fusion.2), channel_id=1, replica_groups=mesh['sta'=8,'win'=4] {'win'}, dimensions={1}, use_global_device_ids=true | all-gather | bytes 5120 | tf_op jit(solution)/shard_map/all_gather | solution.py:90
  355.0 9.4 %multiply_reduce_fusion.1 = (bf16[32,512]{1,0:T(8,128)(2,1)S(1)}, f32[32,512]{1,0:T(8,128)S(1)}) fusion(f32[32,32]{1,0:T(8,128)S(1)} %copy.29, s32[512]{0:T(512)S(1)} %iota_add_fusion, s32[32,32]{1,0:T(8,128)S(1)} %copy.23), kind=kLoop, calls=%fused_computation.30 | loop fusion | flops 9404416 | bytes 108544 | tf_op jit(solution)/shard_map/reduce_sum | solution.py:22
  364.4 11.0 %all_gather.19 = bf16[256,1024]{1,0:T(8,128)(2,1)S(1)} all-gather(bf16[32,1024]{1,0:T(8,128)(2,1)S(1)} %pad_maximum_fusion.4), channel_id=1, replica_groups=mesh['sta'=8,'win'=4] {'sta'}, dimensions={0}, use_global_device_ids=true | all-gather | bytes 589824 | tf_op jit(solution)/shard_map/all_gather | solution.py:92
  376.1 0.7 multiply_reduce_fusion.4
  376.8 38.4 %psum.46 = f32[]{:T(128)} all-reduce(f32[]{:T(128)} %get-tuple-element.26), channel_id=1, replica_groups=mesh['sta'=8,'win'=4] {'sta','win'}, use_global_device_ids=true, to_apply=%region_27.28 | all-reduce | flops 1 | bytes 8 | tf_op jit(solution)/shard_map/psum | solution.py:74
  416.6 1.1 pad_maximum_fusion.2
  417.8 36.9 %reduce-scatter.8.cloned.1.call-done = f32[32,1024]{1,0:T(8,128)} async-done(((f32[256,1024]{1,0:T(8,128)}), f32[32,1024]{1,0:T(8,128)}) %reduce-scatter.8.cloned.1.call-update) | async-done | bytes 131088 | tf_op jit(solution)/shard_map/reduce_scatter | solution.py:67
  454.8 0.9 fusion.36
  455.7 9.7 %subtract_reduce_fusion = f32[32,32]{1,0:T(8,128)S(1)} fusion(f32[32,512]{1,0:T(8,128)S(1)} %get-tuple-element.35, f32[32,512]{1,0:T(8,128)S(1)} %get-tuple-element.34, s32[512]{0:T(512)S(1)} %iota_add_fusion, s32[32,32]{1,0:T(8,128)S(1)} %copy.23), kind=kLoop, calls=%fused_computation.28 | loop fusion | flops 9436160 | bytes 141312 | tf_op jit(solution)/shard_map/reduce_sum | solution.py:31
  465.4 18.7 %all-reduce.2 = f32[32,32]{0,1:T(8,128)S(1)} all-reduce(f32[32,32]{0,1:T(8,128)S(1)} %copy.30), channel_id=7, replica_groups=mesh['sta'=8,'win'=4] {'win'}, use_global_device_ids=true, to_apply=%region_32.33.clone | all-reduce | flops 1024 | bytes 8192
  485.3 37.0 %psum.47 = f32[]{:T(128)} all-reduce(f32[]{:T(128)} %multiply_reduce_fusion.7), channel_id=1, replica_groups=mesh['sta'=8,'win'=4] {'sta','win'}, use_global_device_ids=true, to_apply=%region_34.35 | all-reduce | flops 1 | bytes 8 | tf_op jit(solution)/shard_map/psum | solution.py:77
  (46 shorter events, 8.4 us)
Async XLA Ops:
  7.2 85.0 %reduce-scatter.4.cloned.1.call-start = ((), (), s32[]{:S(2)}) async-start(), calls=%async_computation.3 | async-start | bytes 1179648 | tf_op jit(solution)/shard_map/reduce_scatter | solution.py:67
  54.9 1.2 copy-start.2
  55.0 14.5 %copy-start.3 = (u32[32]{0:T(128)S(1)}, u32[32]{0:T(128)}, u32[]{:S(2)}) copy-start(u32[32]{0:T(128)} %constant.32) | copy-start | bytes 388
  56.1 217.4 %reduce-scatter.6.cloned.1.call-start = ((), (), s32[]{:S(2)}) async-start(), calls=%async_computation.4 | async-start | bytes 1179648 | tf_op jit(solution)/shard_map/reduce_scatter | solution.py:67
  183.1 11.1 %copy-start = (bf16[1,3,2,256,512]{4,3,2,1,0:T(8,128)(2,1)S(1)}, bf16[1,3,2,256,512]{4,3,2,1,0:T(8,128)(2,1)}, u32[]{:S(2)}) copy-start(bf16[1,3,2,256,512]{4,3,2,1,0:T(8,128)(2,1)} %param.4) | copy-start | bytes 4718596
  194.2 0.7 copy-start.1
  236.4 218.4 %reduce-scatter.8.cloned.1.call-start = ((), (), s32[]{:S(2)}) async-start(), calls=%async_computation.5 | async-start | bytes 1179648 | tf_op jit(solution)/shard_map/reduce_scatter | solution.py:67
Sparse Core Ops, SparseCore 0:
  56.2 35.9 reduce-scatter.3
  236.5 36.9 reduce-scatter.5
  417.8 36.9 reduce-scatter.7
where the time goes:
time: 533 us; the launch traced here: 530 us
  blocking collectives  349 us (65%)
  waiting for transfers between devices  95.4 us (18%)
  other arithmetic  62.3 us (12%)
  between operations  19.2 us (4%)
    psum x3, blocking collectives, data_size(): return jnp.sqrt(lax.psum(jnp.sum(left * left), ('sta', 'win')))  119 us
    psum x3, blocking collectives, model_size(): return jnp.sqrt(lax.psum(jnp.sum(right * right), ('sta', 'win')))  111 us
    reduce_scatter x3, waiting for transfers between devices, apply_adjoint(): lax.psum_scatter(back_project(green, rounded), 'sta', scatter_dimension=0...  95.3 us
    unnamed x3, blocking collectives  56.2 us
    reduce_sum x3, other arithmetic, project_with(): jnp.sum(cosine * comb_re[:, None, :] - sine * comb_im[:, None, :], axis=2)  29 us
    all_gather x2, blocking collectives, local(): apply_rows = lax.all_gather(right, 'win', axis=1, tiled=True)  27.6 us
    all_gather x2, blocking collectives, local(): data = contract(green, lax.all_gather(spectrum, 'sta', axis=0, tiled=True))  21.9 us
    reduce_sum x2, other arithmetic, spectra_from(): real_part = jnp.sum(values[:, :, None] * cosine, axis=1)  18.7 us
  transfers between devices with their start and end apart: 3, of which 3 were waited for; matrix products, arithmetic and copies ran while one was open for 0% of the time, Pallas kernels for 0%

commit v1 on v0

v1 whole, which is shorter than its diff:
```python
import functools
import math

import jax
import jax.numpy as jnp
from jax import lax
from jax.experimental import pallas as pl
from jax.experimental.pallas import tpu as pltpu
from jax.sharding import PartitionSpec as P

SAMPLES = 4096
ITERS = 2
LANES = 128
ROWS = 16
GROUP = 4
MESH = pl.DeviceIdType.MESH


def cos_sin(turns):
    quarter = SAMPLES // 4
    shift = quarter.bit_length() - 1
    q = (turns + quarter // 2) >> shift
    x = (turns - (q << shift)).astype(jnp.float32) * (2.0 * math.pi / SAMPLES)
    y = x * x
    s = x + x * y * (-1 / 6 + y * (1 / 120 + y * (-1 / 5040 + y * (1 / 362880))))
    c = 1.0 + y * (-0.5 + y * (1 / 24 + y * (-1 / 720 + y * (1 / 40320))))
    odd = (q & 1) == 1
    cosine = jnp.where(odd, s, c)
    sine = jnp.where(odd, c, s)
    cosine = jnp.where(((q + 1) & 2) == 2, -cosine, cosine)
    sine = jnp.where((q & 2) == 2, -sine, sine)
    return cosine, sine


def kernel(cfg, green, rec, wrow, onset, est_out, dir_out, mis_out,
           on_recv, on_all, on_row, cos_t, sin_t, cd, cd_row, coef, qbuf, u, right, send, recv, piece, full,
           send_sem, recv_sem):
    nsta, nwin, patches, windows, bins, comps, local_w, local_p = cfg
    ndev = nsta * nwin
    nblk = bins // LANES
    npair = nblk // 2
    tiles = patches // LANES
    split = ndev // windows
    width = patches // split
    per_tile = LANES // local_p
    sta, win = lax.axis_index("sta"), lax.axis_index("win")
    me = sta * nwin + win

    def peer(k):
        other = lax.rem(me + k, ndev)
        return {"sta": other // nwin, "win": lax.rem(other, nwin)}, other

    barrier = pltpu.get_barrier_semaphore()

    def greet(k, carry):
        pl.semaphore_signal(barrier, inc=1, device_id=peer(k)[0], device_id_type=MESH)
        return carry

    lax.fori_loop(1, ndev, greet, 0)

    weight = wrow[...]

    def spread_of(src, dst, phase, indexed):
        def one(k, carry):
            where, other = peer(k)
            pltpu.make_async_remote_copy(
                src_ref=src.at[other] if indexed else src.at[0],
                dst_ref=dst.at[me],
                send_sem=send_sem.at[phase],
                recv_sem=recv_sem.at[phase],
                device_id=where,
                device_id_type=MESH,
            ).start()
            return carry
        lax.fori_loop(1, ndev, one, 0)
        pltpu.make_async_copy(src.at[me] if indexed else src.at[0], dst.at[me], recv_sem.at[phase]).start()

    def wait_all(dst, phase):
        pltpu.make_async_copy(dst, dst, recv_sem.at[phase]).wait()
        part = dst.at[pl.ds(0, ndev - 1)]
        pltpu.make_async_copy(part, part, send_sem.at[phase]).wait()

    def green_rows(comp, block, lo):
        rows = pl.ds(pl.multiple_of(block * LANES + lo, ROWS), ROWS)
        return (green[2 * comp, rows, :].astype(jnp.float32),
                green[2 * comp + 1, rows, :].astype(jnp.float32))

    def back_block(block, lo):
        rows = pl.ds(pl.multiple_of(block * LANES + lo, ROWS), ROWS)
        trace = u[rows, :] * weight
        re = im = None
        for comp in range(comps):
            gr, gi = green_rows(comp, block, lo)
            tr, ti = trace[:, 2 * comp:2 * comp + 1], trace[:, 2 * comp + 1:2 * comp + 2]
            a, b = gr * tr + gi * ti, gr * ti - gi * tr
            re, im = (a, b) if re is None else (re + a, im + b)
        return re, im

    def back_rows(lo):
        rows = pl.ds(lo, ROWS)
        for i in range(npair):
            ure, uim = back_block(npair + i, lo)
            lre, lim = back_block(npair - 1 - i, lo)
            qbuf[4 * i, rows, :] = ure + lre
            qbuf[4 * i + 1, rows, :] = uim + lim
            qbuf[4 * i + 2, rows, :] = ure - lre
            qbuf[4 * i + 3, rows, :] = uim - lim

    def project(norm2):
        def group(g, carry):
            for t in range(tiles):
                lanes = slice(t * LANES, (t + 1) * LANES)
                acc = [[None] * (2 * npair) for _ in range(GROUP)]
                for lb in range(LANES // 8):
                    rows = slice(lb * 8, lb * 8 + 8)
                    q = [qbuf[j, rows, lanes] for j in range(4 * npair)]
                    for j in range(GROUP):
                        c = cos_t[g * GROUP + j, rows, lanes]
                        s = sin_t[g * GROUP + j, rows, lanes]
                        for i in range(npair):
                            x = c * q[4 * i] - s * q[4 * i + 1]
                            y = c * q[4 * i + 3] + s * q[4 * i + 2]
                            if lb:
                                x, y = acc[j][2 * i] + x, acc[j][2 * i + 1] + y
                            acc[j][2 * i], acc[j][2 * i + 1] = x, y
                for j in range(GROUP):
                    w = g * GROUP + j
                    total = None
                    for i in range(npair):
                        part = (cd_row[2 * i, w, :, lanes] * acc[j][2 * i]
                                - cd_row[2 * i + 1, w, :, lanes] * acc[j][2 * i + 1])
                        total = part if total is None else total + part
                    row = jnp.sum(total, axis=0, keepdims=True)
                    at = t * LANES
                    send[w * split + at // width, :, at % width:at % width + LANES] = row
            return carry
        lax.fori_loop(0, windows // GROUP, group, 0)
        send[:, :, width:] = jnp.broadcast_to(norm2.reshape(1, 1, 1), (ndev, 1, LANES))

    def all_reduce(turn):
        spread_of(send, recv.at[turn], 1 + 2 * turn, True)
        wait_all(recv.at[turn], 1 + 2 * turn)
        summed = jnp.sum(recv[turn], axis=0)
        piece[0] = summed[:, :width]
        spread_of(piece, full.at[turn], 2 + 2 * turn, False)
        wait_all(full.at[turn], 2 + 2 * turn)
        return summed[:, width:width + 1]

    def image(turn):
        for d in range(ndev):
            at = d % split * width
            right[d // split:d // split + 1, at:at + width] = full[turn, d]
        return right[...]

    def square_sum(x):
        return jnp.sum(jnp.sum(x * x, axis=0, keepdims=True), axis=1, keepdims=True)

    u[...] = rec[...] * weight
    first_norm = square_sum(u[...])

    pl.semaphore_wait(barrier, ndev - 1)
    spread_of(onset, on_recv, 0, False)

    def first(step, carry):
        back_rows(pl.multiple_of(step * ROWS, ROWS))
        return carry
    lax.fori_loop(0, LANES // ROWS, first, 0)

    wait_all(on_recv, 0)
    for z in range(nwin):
        for t in range(tiles):
            block = on_recv[(t * per_tile) * nwin + z]
            for s in range(1, per_tile):
                block = block + on_recv[(t * per_tile + s) * nwin + z]
            on_all[z * local_w:(z + 1) * local_w, t * LANES:(t + 1) * LANES] = block
    for i in range(npair):
        c, s = cos_sin(on_all[...] * (LANES // 2 + i * LANES))
        cd[2 * i], cd[2 * i + 1] = c, s
        for w in range(windows):
            cd_row[2 * i, w], cd_row[2 * i + 1, w] = c[w:w + 1], s[w:w + 1]
    for w in range(windows):
        on_row[w] = on_all[w:w + 1, :]
    centre = win * bins + (bins - LANES) // 2

    def tables(w, carry):
        rowv = on_row[w]
        for lb in range(LANES // ROWS):
            freq = lax.broadcasted_iota(jnp.int32, (ROWS, patches), 0) + (centre + lb * ROWS)
            c, s = cos_sin(freq * rowv)
            cos_t[w, lb * ROWS:(lb + 1) * ROWS, :] = c
            sin_t[w, lb * ROWS:(lb + 1) * ROWS, :] = s
        return carry
    lax.fori_loop(0, windows, tables, 0)

    project(first_norm)
    norm2 = all_reduce(0)
    beta = jnp.sqrt(norm2)
    v = image(0) / beta
    alpha = jnp.sqrt(square_sum(v))
    v = v / alpha
    search = v
    estimate = jnp.zeros_like(v)
    phi_bar, rho_bar = beta, alpha

    for sweep in range(ITERS):
        for i in range(npair):
            coef[2 * i] = v * cd[2 * i]
            coef[2 * i + 1] = v * cd[2 * i + 1]
        right[...] = v

        def forward(step, carry, alpha=alpha, beta=beta):
            lo = pl.multiple_of(step * ROWS, ROWS)
            spectra = [[] for _ in range(2 * nblk)]
            for t in range(tiles):
                lanes = slice(t * LANES, (t + 1) * LANES)
                acc = None
                for w in range(windows):
                    c = cos_t[w, pl.ds(lo, ROWS), lanes]
                    s = sin_t[w, pl.ds(lo, ROWS), lanes]
                    terms = []
                    for i in range(2 * npair):
                        a = coef[i, w:w + 1, lanes]
                        terms += [a * c, a * s]
                    acc = terms if acc is None else [x + y for x, y in zip(acc, terms)]
                for i in range(npair):
                    x1, x2, y1, y2 = acc[4 * i:4 * i + 4]
                    up, low = npair + i, npair - 1 - i
                    spectra[2 * up].append(x1 - y2)
                    spectra[2 * up + 1].append(-x2 - y1)
                    spectra[2 * low].append(x1 + y2)
                    spectra[2 * low + 1].append(y1 - x2)
            lane = lax.broadcasted_iota(jnp.int32, (ROWS, LANES), 1)
            for block in range(nblk):
                sre, sim = [[x.astype(jnp.bfloat16).astype(jnp.float32) for x in spectra[2 * block + k]] for k in range(2)]
                data = jnp.zeros((ROWS, LANES), jnp.float32)
                for comp in range(comps):
                    gr, gi = green_rows(comp, block, lo)
                    re = im = 0.0
                    for t in range(tiles):
                        lanes = slice(t * LANES, (t + 1) * LANES)
                        re = re + (gr[:, lanes] * sre[t] - gi[:, lanes] * sim[t])
                        im = im + (gr[:, lanes] * sim[t] + gi[:, lanes] * sre[t])
                    data = jnp.where(lane == 2 * comp, jnp.sum(re, axis=1, keepdims=True), data)
                    data = jnp.where(lane == 2 * comp + 1, jnp.sum(im, axis=1, keepdims=True), data)
                rows = pl.ds(pl.multiple_of(block * LANES + lo, ROWS), ROWS)
                u[rows, :] = data * weight - (alpha / beta) * u[rows, :]
            back_rows(lo)
            return carry
        lax.fori_loop(0, LANES // ROWS, forward, 0)

        project(square_sum(u[...]))
        norm2 = all_reduce(1 + sweep)
        old = right[...]
        beta = jnp.sqrt(norm2)
        v = image(1 + sweep) / beta - beta * old
        alpha = jnp.sqrt(square_sum(v))
        v = v / alpha
        rho = jnp.sqrt(rho_bar * rho_bar + beta * beta)
        cosine_rot = rho_bar / rho
        sine_rot = beta / rho
        theta = sine_rot * alpha
        rho_bar = -cosine_rot * alpha
        phi = cosine_rot * phi_bar
        phi_bar = sine_rot * phi_bar
        estimate = estimate + phi / rho * search
        search = v - theta / rho * search
    est_out[...] = estimate
    dir_out[...] = search * math.sqrt(patches * windows)
    mis_out[...] = (phi_bar / beta) * u[...]


def local(nsta, nwin, green, records, onsets, mask):
    local_p, local_w = onsets.shape
    comps = green.shape[1]
    patches, windows = local_p * nsta, local_w * nwin
    bins = green.shape[4]
    ndev = nsta * nwin
    width = patches * windows // ndev
    npair = bins // LANES // 2
    columns = 2 * comps
    green_t = jnp.swapaxes(green.reshape(columns, patches, bins), 1, 2)
    rec = jnp.pad(records.reshape(columns, bins).T, ((0, 0), (0, LANES - columns)))
    weight = jnp.pad(jnp.repeat(mask.astype(jnp.float32), 2, axis=1), ((0, 0), (0, LANES - columns)))
    sta, win = lax.axis_index("sta"), lax.axis_index("win")
    group = LANES // local_p
    mine = jnp.arange(LANES) // local_p == sta % group
    onset = jnp.where(mine[None, :], jnp.tile(onsets.T, (1, group)), 0)[None]
    cfg = (nsta, nwin, patches, windows, bins, comps, local_w, local_p)
    f32 = jnp.float32
    turns = ITERS + 1
    est, direction, misfit = pl.pallas_call(
        functools.partial(kernel, cfg),
        out_shape=(jax.ShapeDtypeStruct((windows, patches), f32),
                   jax.ShapeDtypeStruct((windows, patches), f32),
                   jax.ShapeDtypeStruct((bins, LANES), f32)),
        in_specs=[pl.BlockSpec(memory_space=pltpu.VMEM)] * 4,
        out_specs=(pl.BlockSpec(memory_space=pltpu.VMEM),) * 3,
        scratch_shapes=[
            pltpu.VMEM((ndev, local_w, LANES), jnp.int32),
            pltpu.VMEM((windows, patches), jnp.int32),
            pltpu.VMEM((windows, 1, patches), jnp.int32),
            pltpu.VMEM((windows, LANES, patches), f32),
            pltpu.VMEM((windows, LANES, patches), f32),
            pltpu.VMEM((2 * npair, windows, patches), f32),
            pltpu.VMEM((2 * npair, windows, 1, patches), f32),
            pltpu.VMEM((2 * npair, windows, patches), f32),
            pltpu.VMEM((4 * npair, LANES, patches), f32),
            pltpu.VMEM((bins, LANES), f32),
            pltpu.VMEM((windows, patches), f32),
            pltpu.VMEM((ndev, 1, width + LANES), f32),
            pltpu.VMEM((turns, ndev, 1, width + LANES), f32),
            pltpu.VMEM((1, 1, width), f32),
            pltpu.VMEM((turns, ndev, 1, width), f32),
            pltpu.SemaphoreType.DMA((1 + 2 * turns,)),
            pltpu.SemaphoreType.DMA((1 + 2 * turns,)),
        ],
        compiler_params=pltpu.CompilerParams(
            collective_id=0, has_side_effects=True, vmem_limit_bytes=56 * 2**20),
    )(green_t, rec, weight, onset)
    def mine_of(x):
        return lax.dynamic_slice(x, (win * local_w, sta * local_p), (local_w, local_p)).T
    left = misfit[:, :columns].T.reshape(1, comps, 2, bins)
    return mine_of(est), mine_of(direction), left


def solution(mesh):
    return jax.shard_map(
        functools.partial(local, mesh.shape["sta"], mesh.shape["win"]),
        mesh=mesh,
        in_specs=(
            P("sta", None, None, None, "win"),
            P("sta", None, None, "win"),
            P("sta", "win"),
            P("sta", None),
        ),
        out_specs=(P("sta", "win"), P("sta", "win"), P("sta", None, None, "win")),
        check_vma=False,
    )
```

time: 533 us -> 76.3 us (0.14)
  blocking collectives: 349 us -> 0 us
  waiting for transfers between devices: 95.4 us -> 0 us
  Pallas kernels: 0 us -> 65.4 us
  other arithmetic: 62.3 us -> 1.27 us
  between operations: 19.2 us -> 0.68 us
    psum x6 -> x0, blocking collectives: 230 us -> none  [the longest x3 119 us: data_size(): return jnp.sqrt(lax.psum(jnp.sum(left * left), ('sta', 'win')))]
    reduce_scatter x3 -> x0, waiting for transfers between devices: 95.3 us -> none  [apply_adjoint(): lax.psum_scatter(back_project(green, rounded), 'sta', scatter_dimension=0...]
    pallas_call x0 -> x1, Pallas kernels: none -> 65.4 us  [local(): pl.pallas_call(functools.partial(kernel, cfg), out_shape=(jax.ShapeDtypeS...]
    all_gather x5 -> x0, blocking collectives: 62.7 us -> none  [the longest x2 27.6 us: local(): apply_rows = lax.all_gather(right, 'win', axis=1, tiled=True)]
    reduce_sum x16 -> x0, other arithmetic: 56.5 us -> none  [the longest x3 29 us: project_with(): jnp.sum(cosine * comb_re[:, None, :] - sine * comb_im[:, None, :], axis=2)]
    unnamed x3 -> x0, blocking collectives: 56.2 us -> none
  transfers between devices with their start and end apart: 3 -> 0, of which waited for: 3 -> 0; matrix products, arithmetic and copies ran while one was open for 0% -> 0% of each run, Pallas kernels for 0% -> 0%
where the time goes in v1:
time: 76.3 us; the launch traced here: 76 us
  Pallas kernels  65.4 us (86%)
  local copies, waits for them, and re-layouts  8.72 us (11%)
  other arithmetic  1.27 us (2%)
    pallas_call x1, Pallas kernels, local(): pl.pallas_call(functools.partial(kernel, cfg), out_shape=(jax.ShapeDtypeS...  65.4 us
    unnamed x1, local copies, waits for them, and re-layouts  2.61 us

profile of v1, /device:TPU:0, one launch (start us, length us, event | category | flops | bytes accessed | tf_op | source)
XLA Modules:
  0.0 76.0 jit_solution(2019514995087240324)
XLA Ops:
  0.7 0.7 convert_bitcast_fusion
  1.3 0.1 broadcast_in_dim.19
  1.4 0.1 broadcast_in_dim.20
  1.5 0.5 pad.9.wrow
  2.0 0.7 reshape.72
  2.7 0.7 tile.4
  3.4 0.1 tile.10
  3.5 0.6 broadcast_select_fusion.onset
  4.1 0.1 copy.11
  4.2 0.7 pad.8.rec
  5.0 2.6 %copy.10 = bf16[1,3,2,256,512]{3,4,2,1,0:T(8,128)(2,1)} copy(bf16[1,3,2,256,512]{4,3,2,1,0:T(8,128)(2,1)} %param.4) | data formatting | bytes 3145728 | tf_op args[0]
  7.6 65.4 %shard_map.67 = (f32[32,256]{1,0:T(8,128)}, f32[32,256]{1,0:T(8,128)}, f32[512,128]{1,0:T(8,128)}) custom-call(bf16[6,512,256]{2,1,0:T(8,128)(2,1)} %bitcast.13, f32[512,128]{1,0:T(8,128)} %pad.8.rec, f32[1,128]{1,0:T(1,128)} %pad.9.wrow, s32[1,8,128]{2,1,0:T(8,128)} %broadcast_select_fusion.onset), custom_call_target="tpu_custom_call" | custom-call | tf_op jit(solution)/shard_map/pallas_call | solution.py:291
  72.9 1.4 %dynamic-slice_bitcast_fusion = (f32[32,8]{0,1:T(8,128)}, f32[32,8]{0,1:T(8,128)}) fusion(f32[32,256]{1,0:T(8,128)} %get-tuple-element.7, s32[]{:T(128)S(6)} %select_n.38, s32[]{:T(128)S(6)} %select_n.39, f32[32,256]{1,0:T(8,128)} %get-tuple-element.6), kind=kLoop, calls=%fused_computation.1 | loop fusion | bytes 4104 | tf_op jit(solution)/shard_map/transpose | solution.py:321
  74.3 1.0 %slice_bitcast_fusion = f32[6,512]{0,1:T(8,128)S(1)} fusion(f32[512,128]{1,0:T(8,128)} %get-tuple-element.8), kind=kLoop, calls=%fused_computation | loop fusion | bytes 24576 | tf_op jit(solution)/shard_map/transpose | solution.py:322
  75.3 0.1 copy.12
  75.4 0.6 reshape.73
  (1 shorter events, 0.0 us)

commit v2 on v1

--- a/solution.py
+++ b/solution.py
@@ -32,8 +32,8 @@
     return cosine, sine
 
 
-def kernel(cfg, green, rec, wrow, onset, est_out, dir_out, mis_out,
-           on_recv, on_all, on_row, cos_t, sin_t, cd, cd_row, coef, qbuf, u, right, send, recv, piece, full,
+def kernel(cfg, green_in, rec, onset_in, mask, est_out, dir_out, mis_out,
+           green_raw, green, green_sem, tmp, onset, on_recv, on_all, on_row, cos_t, sin_t, cd, cd_row, coef, qbuf, u, right, turned, send, recv, piece, full,
            send_sem, recv_sem):
     nsta, nwin, patches, windows, bins, comps, local_w, local_p = cfg
     ndev = nsta * nwin
@@ -46,34 +46,36 @@
     sta, win = lax.axis_index("sta"), lax.axis_index("win")
     me = sta * nwin + win
 
-    def peer(k):
-        other = lax.rem(me + k, ndev)
-        return {"sta": other // nwin, "win": lax.rem(other, nwin)}, other
+    def wrapped(x, size):
+        return jnp.where(x >= size, x - size, x)
+
+    stas = [wrapped(sta + k, nsta) for k in range(nsta)]
+    wins = [wrapped(win + k, nwin) for k in range(nwin)]
+    near = sorted(range(nwin), key=lambda k: -min(k, nwin - k))
+    peers = [(stas[a], wins[b]) for b in near for a in range(nsta - 1, -1, -1) if a or b]
 
     barrier = pltpu.get_barrier_semaphore()
-
-    def greet(k, carry):
-        pl.semaphore_signal(barrier, inc=1, device_id=peer(k)[0], device_id_type=MESH)
-        return carry
-
-    lax.fori_loop(1, ndev, greet, 0)
-
-    weight = wrow[...]
-
-    def spread_of(src, dst, phase, indexed):
-        def one(k, carry):
-            where, other = peer(k)
-            pltpu.make_async_remote_copy(
-                src_ref=src.at[other] if indexed else src.at[0],
-                dst_ref=dst.at[me],
-                send_sem=send_sem.at[phase],
-                recv_sem=recv_sem.at[phase],
-                device_id=where,
-                device_id_type=MESH,
-            ).start()
-            return carry
-        lax.fori_loop(1, ndev, one, 0)
-        pltpu.make_async_copy(src.at[me] if indexed else src.at[0], dst.at[me], recv_sem.at[phase]).start()
+    for other_sta, other_win in peers:
+        pl.semaphore_signal(barrier, inc=1, device_id={"sta": other_sta, "win": other_win},
+                            device_id_type=MESH)
+    green_copy = pltpu.make_async_copy(green_in, green_raw, green_sem)
+    green_copy.start()
+
+    lane_row = lax.broadcasted_iota(jnp.int32, (1, LANES), 1)
+    weight = jnp.zeros((1, LANES), jnp.float32)
+    for comp in range(comps):
+        on = jnp.full((1, LANES), mask[0, comp], jnp.int32).astype(jnp.float32)
+        weight = jnp.where(lane_row // 2 == comp, on, weight)
+
+    def remote(src, dst, phase, other_sta, other_win):
+        return pltpu.make_async_remote_copy(
+            src_ref=src, dst_ref=dst, send_sem=send_sem.at[phase], recv_sem=recv_sem.at[phase],
+            device_id={"sta": other_sta, "win": other_win}, device_id_type=MESH)
+
+    def spread(src, dst, phase):
+        for other_sta, other_win in peers:
+            remote(src.at[0], dst.at[me], phase, other_sta, other_win).start()
+        pltpu.make_async_copy(src.at[0], dst.at[me], recv_sem.at[phase]).start()
 
     def wait_all(dst, phase):
         pltpu.make_async_copy(dst, dst, recv_sem.at[phase]).wait()
@@ -106,7 +108,9 @@
             qbuf[4 * i + 2, rows, :] = ure - lre
             qbuf[4 * i + 3, rows, :] = uim - lim
 
-    def project(norm2):
+    def project(norm2, turn):
+        norm_row = jnp.broadcast_to(norm2, (1, LANES))
+
         def group(g, carry):
             for t in range(tiles):
                 lanes = slice(t * LANES, (t + 1) * LANES)
@@ -133,16 +137,26 @@
                     row = jnp.sum(total, axis=0, keepdims=True)
                     at = t * LANES
                     send[w * split + at // width, :, at % width:at % width + LANES] = row
+            for j in range(GROUP * split):
+                d = g * (GROUP * split) + j
+                send[d, :, width:] = norm_row
+                phase = 1 + 2 * turn
+
+                @pl.when(d != me)
+                def _():
+                    remote(send.at[d], recv.at[turn, me], phase, d // nwin, lax.rem(d, nwin)).start()
+
+                @pl.when(d == me)
+                def _():
+                    pltpu.make_async_copy(send.at[d], recv.at[turn, me], recv_sem.at[phase]).start()
             return carry
         lax.fori_loop(0, windows // GROUP, group, 0)
-        send[:, :, width:] = jnp.broadcast_to(norm2.reshape(1, 1, 1), (ndev, 1, LANES))
 
     def all_reduce(turn):
-        spread_of(send, recv.at[turn], 1 + 2 * turn, True)
         wait_all(recv.at[turn], 1 + 2 * turn)
         summed = jnp.sum(recv[turn], axis=0)
         piece[0] = summed[:, :width]
-        spread_of(piece, full.at[turn], 2 + 2 * turn, False)
+        spread(piece, full.at[turn], 2 + 2 * turn)
         wait_all(full.at[turn], 2 + 2 * turn)
         return summed[:, width:width + 1]
 
@@ -155,11 +169,29 @@
     def square_sum(x):
         return jnp.sum(jnp.sum(x * x, axis=0, keepdims=True), axis=1, keepdims=True)
 
-    u[...] = rec[...] * weight
+    tmp[:, 0:LANES] = jnp.zeros((LANES, LANES), jnp.float32)
+    start = pl.multiple_of(lax.rem(sta, per_tile) * local_p, local_p)
+    tmp[pl.ds(start, local_p), 0:local_w] = onset_in[...].astype(jnp.float32)
+    onset[0] = tmp[:, 0:LANES].T[0:local_w, :]
+    pl.semaphore_wait(barrier, ndev - 1)
+    spread(onset, on_recv, 0)
+
+    tmp[...] = jnp.zeros_like(tmp)
+    for comp in range(comps):
+        for part in range(2):
+            tmp[2 * comp + part:2 * comp + part + 1, 0:bins] = rec[0, comp, part:part + 1, :]
+    for block in range(nblk):
+        lanes = slice(block * LANES, (block + 1) * LANES)
+        u[lanes, :] = tmp[:, lanes].T * weight
     first_norm = square_sum(u[...])
-
-    pl.semaphore_wait(barrier, ndev - 1)
-    spread_of(onset, on_recv, 0, False)
+    green_copy.wait()
+    for comp in range(comps):
+        for part in range(2):
+            for block in range(nblk):
+                rows = slice(block * LANES, (block + 1) * LANES)
+                for t in range(tiles):
+                    lanes = slice(t * LANES, (t + 1) * LANES)
+                    green[2 * comp + part, rows, lanes] = green_raw[0, comp, part, lanes, rows].T
 
     def first(step, carry):
         back_rows(pl.multiple_of(step * ROWS, ROWS))
@@ -172,7 +204,7 @@
             block = on_recv[(t * per_tile) * nwin + z]
             for s in range(1, per_tile):
                 block = block + on_recv[(t * per_tile + s) * nwin + z]
-            on_all[z * local_w:(z + 1) * local_w, t * LANES:(t + 1) * LANES] = block
+            on_all[z * local_w:(z + 1) * local_w, t * LANES:(t + 1) * LANES] = block.astype(jnp.int32)
     for i in range(npair):
         c, s = cos_sin(on_all[...] * (LANES // 2 + i * LANES))
         cd[2 * i], cd[2 * i + 1] = c, s
@@ -184,15 +216,20 @@
 
     def tables(w, carry):
         rowv = on_row[w]
-        for lb in range(LANES // ROWS):
-            freq = lax.broadcasted_iota(jnp.int32, (ROWS, patches), 0) + (centre + lb * ROWS)
-            c, s = cos_sin(freq * rowv)
-            cos_t[w, lb * ROWS:(lb + 1) * ROWS, :] = c
-            sin_t[w, lb * ROWS:(lb + 1) * ROWS, :] = s
+        low = lax.broadcasted_iota(jnp.int32, (ROWS, patches), 0) + centre
+        c0, s0 = cos_sin(low * rowv)
+        high = lax.broadcasted_iota(jnp.int32, (LANES // ROWS, patches), 0) * ROWS
+        c1, s1 = cos_sin(high * rowv)
+        cos_t[w, 0:ROWS, :] = c0
+        sin_t[w, 0:ROWS, :] = s0
+        for lb in range(1, LANES // ROWS):
+            ch, sh = c1[lb:lb + 1], s1[lb:lb + 1]
+            cos_t[w, lb * ROWS:(lb + 1) * ROWS, :] = c0 * ch - s0 * sh
+            sin_t[w, lb * ROWS:(lb + 1) * ROWS, :] = s0 * ch + c0 * sh
         return carry
     lax.fori_loop(0, windows, tables, 0)
 
-    project(first_norm)
+    project(first_norm, 0)
     norm2 = all_reduce(0)
     beta = jnp.sqrt(norm2)
     v = image(0) / beta
@@ -248,7 +285,7 @@
             return carry
         lax.fori_loop(0, LANES // ROWS, forward, 0)
 
-        project(square_sum(u[...]))
+        project(square_sum(u[...]), 1 + sweep)
         norm2 = all_reduce(1 + sweep)
         old = right[...]
         beta = jnp.sqrt(norm2)
@@ -264,9 +301,23 @@
         phi_bar = sine_rot * phi_bar
         estimate = estimate + phi / rho * search
         search = v - theta / rho * search
-    est_out[...] = estimate
-    dir_out[...] = search * math.sqrt(patches * windows)
-    mis_out[...] = (phi_bar / beta) * u[...]
+    tmp[...] = jnp.zeros_like(tmp)
+    for value, out in ((estimate, est_out), (search * math.sqrt(patches * windows), dir_out)):
+        tmp[0:windows, 0:patches] = value
+        for t in range(tiles):
+            lanes = slice(t * LANES, (t + 1) * LANES)
+            turned[lanes, :] = tmp[:, lanes].T
+        rows = turned[pl.ds(pl.multiple_of(sta * local_p, local_p), local_p), :]
+        own = rows[:, 0:local_w]
+        for z in range(1, nwin):
+            own = jnp.where(win == z, rows[:, z * local_w:(z + 1) * local_w], own)
+        out[...] = own
+    scale = phi_bar / beta
+    for block in range(nblk):
+        lanes = slice(block * LANES, (block + 1) * LANES)
+        flipped = (u[lanes, :] * scale).T
+        for comp in range(comps):
+            mis_out[0, comp, :, lanes] = flipped[2 * comp:2 * comp + 2, :]
 
 
 def local(nsta, nwin, green, records, onsets, mask):
@@ -277,26 +328,26 @@
     ndev = nsta * nwin
     width = patches * windows // ndev
     npair = bins // LANES // 2
-    columns = 2 * comps
-    green_t = jnp.swapaxes(green.reshape(columns, patches, bins), 1, 2)
-    rec = jnp.pad(records.reshape(columns, bins).T, ((0, 0), (0, LANES - columns)))
-    weight = jnp.pad(jnp.repeat(mask.astype(jnp.float32), 2, axis=1), ((0, 0), (0, LANES - columns)))
-    sta, win = lax.axis_index("sta"), lax.axis_index("win")
-    group = LANES // local_p
-    mine = jnp.arange(LANES) // local_p == sta % group
-    onset = jnp.where(mine[None, :], jnp.tile(onsets.T, (1, group)), 0)[None]
     cfg = (nsta, nwin, patches, windows, bins, comps, local_w, local_p)
     f32 = jnp.float32
     turns = ITERS + 1
-    est, direction, misfit = pl.pallas_call(
+    return pl.pallas_call(
         functools.partial(kernel, cfg),
-        out_shape=(jax.ShapeDtypeStruct((windows, patches), f32),
-                   jax.ShapeDtypeStruct((windows, patches), f32),
-                   jax.ShapeDtypeStruct((bins, LANES), f32)),
-        in_specs=[pl.BlockSpec(memory_space=pltpu.VMEM)] * 4,
+        out_shape=(jax.ShapeDtypeStruct((local_p, local_w), f32),
+                   jax.ShapeDtypeStruct((local_p, local_w), f32),
+                   jax.ShapeDtypeStruct((1, comps, 2, bins), f32)),
+        in_specs=[pl.BlockSpec(memory_space=pl.ANY),
+                  pl.BlockSpec(memory_space=pltpu.VMEM),
+                  pl.BlockSpec(memory_space=pltpu.VMEM),
+                  pl.BlockSpec(memory_space=pltpu.SMEM)],
         out_specs=(pl.BlockSpec(memory_space=pltpu.VMEM),) * 3,
         scratch_shapes=[
-            pltpu.VMEM((ndev, local_w, LANES), jnp.int32),
+            pltpu.VMEM((1, comps, 2, patches, bins), jnp.bfloat16),
+            pltpu.VMEM((2 * comps, bins, patches), jnp.bfloat16),
+            pltpu.SemaphoreType.DMA,
+            pltpu.VMEM((LANES, max(bins, patches)), f32),
+            pltpu.VMEM((1, local_w, LANES), f32),
+            pltpu.VMEM((ndev, local_w, LANES), f32),
             pltpu.VMEM((windows, patches), jnp.int32),
             pltpu.VMEM((windows, 1, patches), jnp.int32),
             pltpu.VMEM((windows, LANES, patches), f32),
@@ -307,6 +358,7 @@
             pltpu.VMEM((4 * npair, LANES, patches), f32),
             pltpu.VMEM((bins, LANES), f32),
             pltpu.VMEM((windows, patches), f32),
+            pltpu.VMEM((patches, LANES), f32),
             pltpu.VMEM((ndev, 1, width + LANES), f32),
             pltpu.VMEM((turns, ndev, 1, width + LANES), f32),
             pltpu.VMEM((1, 1, width), f32),
@@ -316,11 +368,7 @@
         ],
         compiler_params=pltpu.CompilerParams(
             collective_id=0, has_side_effects=True, vmem_limit_bytes=56 * 2**20),
-    )(green_t, rec, weight, onset)
-    def mine_of(x):
-        return lax.dynamic_slice(x, (win * local_w, sta * local_p), (local_w, local_p)).T
-    left = misfit[:, :columns].T.reshape(1, comps, 2, bins)
-    return mine_of(est), mine_of(direction), left
+    )(green, records, onsets, mask)
 
 
 def solution(mesh):

time: 76.3 us -> 69.4 us (0.910)
  local copies, waits for them, and re-layouts: 8.72 us -> 5.42 us
  Pallas kernels: 65.4 us -> 62.8 us
  other arithmetic: 1.27 us -> 0 us
    pallas_call x0 -> x2, local copies, waits for them, and re-layouts: none -> 2.76 us  [local(): pl.pallas_call(functools.partial(kernel, cfg), out_shape=(jax.ShapeDtypeS...]
    pallas_call x1, Pallas kernels: 65.4 us -> 62.8 us  [local(): pl.pallas_call(functools.partial(kernel, cfg), out_shape=(jax.ShapeDtypeS...]
    transpose x3 -> x0, local copies, waits for them, and re-layouts: 2.44 us -> none  [the longest x1 1.37 us: mine_of(): lax.dynamic_slice(x, (win * local_w, sta * local_p), (local_w, local_p))]
    reshape x3 -> x0, local copies, waits for them, and re-layouts: 1.49 us -> none  [the longest x2 0.86 us: local(): records.reshape(columns, bins)]
    pad x2 -> x0, local copies, waits for them, and re-layouts: 1.24 us -> none  [the longest x1 0.73 us: local(): jnp.pad(records.reshape(columns, bins).T, ((0, 0), (0, LANES - columns)))]
    another operation x2 -> x0, local copies, waits for them, and re-layouts: 0.77 us -> none  [local(): onset = jnp.where(mine[None, :], jnp.tile(onsets.T, (1, group)), 0)[None]]
    unnamed x1 -> x2, local copies, waits for them, and re-layouts: 2.61 us -> 2.67 us
where the time goes in v2:
time: 69.4 us; the launch traced here: 68.9 us
  Pallas kernels  62.8 us (90%)
  local copies, waits for them, and re-layouts  5.42 us (8%)
    pallas_call x1, Pallas kernels, local(): pl.pallas_call(functools.partial(kernel, cfg), out_shape=(jax.ShapeDtypeS...  62.8 us
    pallas_call x2, local copies, waits for them, and re-layouts, local(): pl.pallas_call(functools.partial(kernel, cfg), out_shape=(jax.ShapeDtypeS...  2.76 us
    unnamed x2, local copies, waits for them, and re-layouts  2.67 us

profile of v2, /device:TPU:0, one launch (start us, length us, event | category | flops | bytes accessed | tf_op | source)
XLA Modules:
  0.0 68.9 jit_solution(16201601319873600064)
XLA Ops:
  0.6 1.4 %copy.7.onset_in = s32[32,8]{1,0:T(8,128)} copy(s32[32,8]{0,1:T(8,128)} %param.6) | data formatting | bytes 2048 | tf_op args[2]
  2.0 62.8 %shard_map.67 = (f32[32,8]{1,0:T(8,128)}, f32[32,8]{1,0:T(8,128)}, f32[1,3,2,512]{3,2,1,0:T(2,128)}) custom-call(bf16[1,3,2,256,512]{4,3,2,1,0:T(8,128)(2,1)} %green_in.1, f32[1,3,2,512]{3,2,1,0:T(2,128)} %rec.1, s32[32,8]{1,0:T(8,128)} %copy.7.onset_in, s32[1,3]{1,0:T(1,128)} %mask.1), custom_call_target="tpu_custom_call" | custom-call | tf_op jit(solution)/shard_map/pallas_call | solution.py:334
  64.8 1.4 %copy.8 = f32[32,8]{0,1:T(8,128)} copy(f32[32,8]{1,0:T(8,128)} %get-tuple-element.3) | data formatting | bytes 2048 | tf_op jit(solution)/shard_map/pallas_call | solution.py:334
  66.2 1.4 %copy.9 = f32[32,8]{0,1:T(8,128)} copy(f32[32,8]{1,0:T(8,128)} %get-tuple-element.4) | data formatting | bytes 2048 | tf_op jit(solution)/shard_map/pallas_call | solution.py:334
  67.6 1.3 %copy.11 = f32[1,3,2,512]{3,2,1,0:T(2,128)} copy(f32[1,3,2,512]{3,2,1,0:T(2,128)} %get-tuple-element.11) | data formatting | bytes 24576

commit v3 on v2

--- a/solution.py
+++ b/solution.py
@@ -12,7 +12,6 @@
 ITERS = 2
 LANES = 128
 ROWS = 16
-GROUP = 4
 MESH = pl.DeviceIdType.MESH
 
 
@@ -32,16 +31,16 @@
     return cosine, sine
 
 
-def kernel(cfg, green_in, rec, onset_in, mask, est_out, dir_out, mis_out,
-           green_raw, green, green_sem, tmp, onset, on_recv, on_all, on_row, cos_t, sin_t, cd, cd_row, coef, qbuf, u, right, turned, send, recv, piece, full,
+def kernel(cfg, green_in, rec_in, onset_in, mask, est_out, dir_out, mis_out,
+           green_raw, green, green_sem, rec, rec_sem, onset_own, onset_sem, tmp, onset, on_recv, on_all, on_row, cos_t, sin_t, cd, cd_row, coef, qbuf, u, right, turned, send, recv, piece, level, total_piece, full,
            send_sem, recv_sem):
     nsta, nwin, patches, windows, bins, comps, local_w, local_p = cfg
     ndev = nsta * nwin
     nblk = bins // LANES
     npair = nblk // 2
     tiles = patches // LANES
-    split = ndev // windows
-    width = patches // split
+    group_rows = windows // nsta
+    width = patches
     per_tile = LANES // local_p
     sta, win = lax.axis_index("sta"), lax.axis_index("win")
     me = sta * nwin + win
@@ -58,6 +57,10 @@
     for other_sta, other_win in peers:
         pl.semaphore_signal(barrier, inc=1, device_id={"sta": other_sta, "win": other_win},
                             device_id_type=MESH)
+    onset_copy = pltpu.make_async_copy(onset_in, onset_own, onset_sem)
+    onset_copy.start()
+    rec_copy = pltpu.make_async_copy(rec_in, rec, rec_sem)
+    rec_copy.start()
     green_copy = pltpu.make_async_copy(green_in, green_raw, green_sem)
     green_copy.start()
 
@@ -72,14 +75,12 @@
             src_ref=src, dst_ref=dst, send_sem=send_sem.at[phase], recv_sem=recv_sem.at[phase],
             device_id={"sta": other_sta, "win": other_win}, device_id_type=MESH)
 
-    def spread(src, dst, phase):
-        for other_sta, other_win in peers:
-            remote(src.at[0], dst.at[me], phase, other_sta, other_win).start()
-        pltpu.make_async_copy(src.at[0], dst.at[me], recv_sem.at[phase]).start()
+    def local_copy(src, dst, phase):
+        return pltpu.make_async_copy(src, dst, recv_sem.at[phase])
 
     def wait_all(dst, phase):
         pltpu.make_async_copy(dst, dst, recv_sem.at[phase]).wait()
-        part = dst.at[pl.ds(0, ndev - 1)]
+        part = dst.at[pl.ds(0, dst.shape[0] - 1)]
         pltpu.make_async_copy(part, part, send_sem.at[phase]).wait()
 
     def green_rows(comp, block, lo):
@@ -114,56 +115,62 @@
         def group(g, carry):
             for t in range(tiles):
                 lanes = slice(t * LANES, (t + 1) * LANES)
-                acc = [[None] * (2 * npair) for _ in range(GROUP)]
+                acc = [[None] * (2 * npair) for _ in range(group_rows)]
                 for lb in range(LANES // 8):
                     rows = slice(lb * 8, lb * 8 + 8)
                     q = [qbuf[j, rows, lanes] for j in range(4 * npair)]
-                    for j in range(GROUP):
-                        c = cos_t[g * GROUP + j, rows, lanes]
-                        s = sin_t[g * GROUP + j, rows, lanes]
+                    for j in range(group_rows):
+                        c = cos_t[g * group_rows + j, rows, lanes]
+                        s = sin_t[g * group_rows + j, rows, lanes]
                         for i in range(npair):
                             x = c * q[4 * i] - s * q[4 * i + 1]
                             y = c * q[4 * i + 3] + s * q[4 * i + 2]
                             if lb:
                                 x, y = acc[j][2 * i] + x, acc[j][2 * i + 1] + y
                             acc[j][2 * i], acc[j][2 * i + 1] = x, y
-                for j in range(GROUP):
-                    w = g * GROUP + j
+                for j in range(group_rows):
+                    w = g * group_rows + j
                     total = None
                     for i in range(npair):
                         part = (cd_row[2 * i, w, :, lanes] * acc[j][2 * i]
                                 - cd_row[2 * i + 1, w, :, lanes] * acc[j][2 * i + 1])
                         total = part if total is None else total + part
                     row = jnp.sum(total, axis=0, keepdims=True)
-                    at = t * LANES
-                    send[w * split + at // width, :, at % width:at % width + LANES] = row
-            for j in range(GROUP * split):
-                d = g * (GROUP * split) + j
-                send[d, :, width:] = norm_row
-                phase = 1 + 2 * turn
-
-                @pl.when(d != me)
-                def _():
-                    remote(send.at[d], recv.at[turn, me], phase, d // nwin, lax.rem(d, nwin)).start()
-
-                @pl.when(d == me)
-                def _():
-                    pltpu.make_async_copy(send.at[d], recv.at[turn, me], recv_sem.at[phase]).start()
+                    send[g, j:j + 1, lanes] = row
+                    if t == 0:
+                        send[g, j:j + 1, width:] = norm_row
+            phase = 1 + 3 * turn
+
+            @pl.when(g != sta)
+            def _():
+                remote(send.at[g], recv.at[turn, sta], phase, g, win).start()
+
+            @pl.when(g == sta)
+            def _():
+                local_copy(send.at[g], recv.at[turn, sta], phase).start()
             return carry
-        lax.fori_loop(0, windows // GROUP, group, 0)
+        lax.fori_loop(0, nsta, group, 0)
 
     def all_reduce(turn):
-        wait_all(recv.at[turn], 1 + 2 * turn)
-        summed = jnp.sum(recv[turn], axis=0)
-        piece[0] = summed[:, :width]
-        spread(piece, full.at[turn], 2 + 2 * turn)
-        wait_all(full.at[turn], 2 + 2 * turn)
-        return summed[:, width:width + 1]
+        phase = 1 + 3 * turn
+        wait_all(recv.at[turn], phase)
+        piece[...] = jnp.sum(recv[turn], axis=0)
+        for b in near:
+            if b:
+                remote(piece, level.at[turn, win], phase + 1, sta, wins[b]).start()
+        local_copy(piece, level.at[turn, win], phase + 1).start()
+        wait_all(level.at[turn], phase + 1)
+        summed = jnp.sum(level[turn], axis=0)
+        total_piece[...] = summed[:, :width]
+        for a in range(nsta - 1, 0, -1):
+            remote(total_piece, full.at[turn, sta], phase + 2, stas[a], win).start()
+        local_copy(total_piece, full.at[turn, sta], phase + 2).start()
+        wait_all(full.at[turn], phase + 2)
+        return summed[0:1, width:width + 1]
 
     def image(turn):
-        for d in range(ndev):
-            at = d % split * width
-            right[d // split:d // split + 1, at:at + width] = full[turn, d]
+        for d in range(nsta):
+            right[d * group_rows:(d + 1) * group_rows, :] = full[turn, d]
         return right[...]
 
     def square_sum(x):
@@ -171,12 +178,18 @@
 
     tmp[:, 0:LANES] = jnp.zeros((LANES, LANES), jnp.float32)
     start = pl.multiple_of(lax.rem(sta, per_tile) * local_p, local_p)
-    tmp[pl.ds(start, local_p), 0:local_w] = onset_in[...].astype(jnp.float32)
-    onset[0] = tmp[:, 0:LANES].T[0:local_w, :]
+    turned[...] = jnp.zeros_like(turned)
+    onset_copy.wait()
+    tmp[0:local_w, 0:local_p] = onset_own[...].astype(jnp.float32)
+    turned[pl.ds(start, LANES), :] = tmp[:, 0:LANES].T
+    onset[...] = turned[0:LANES, :].T[0:local_w, :]
     pl.semaphore_wait(barrier, ndev - 1)
-    spread(onset, on_recv, 0)
+    for other_sta, other_win in peers:
+        remote(onset, on_recv.at[me], 0, other_sta, other_win).start()
+    local_copy(onset, on_recv.at[me], 0).start()
 
     tmp[...] = jnp.zeros_like(tmp)
+    rec_copy.wait()
     for comp in range(comps):
         for part in range(2):
             tmp[2 * comp + part:2 * comp + part + 1, 0:bins] = rec[0, comp, part:part + 1, :]
@@ -307,10 +320,10 @@
         for t in range(tiles):
             lanes = slice(t * LANES, (t + 1) * LANES)
             turned[lanes, :] = tmp[:, lanes].T
-        rows = turned[pl.ds(pl.multiple_of(sta * local_p, local_p), local_p), :]
-        own = rows[:, 0:local_w]
+        rows = turned[pl.ds(pl.multiple_of(sta * local_p, local_p), LANES), :].T
+        own = rows[0:local_w, 0:local_p]
         for z in range(1, nwin):
-            own = jnp.where(win == z, rows[:, z * local_w:(z + 1) * local_w], own)
+            own = jnp.where(win == z, rows[z * local_w:(z + 1) * local_w, 0:local_p], own)
         out[...] = own
     scale = phi_bar / beta
     for block in range(nblk):
@@ -326,27 +339,32 @@
     patches, windows = local_p * nsta, local_w * nwin
     bins = green.shape[4]
     ndev = nsta * nwin
-    width = patches * windows // ndev
+    width = patches
+    group_rows = windows // nsta
     npair = bins // LANES // 2
     cfg = (nsta, nwin, patches, windows, bins, comps, local_w, local_p)
     f32 = jnp.float32
     turns = ITERS + 1
-    return pl.pallas_call(
+    slip, direction, misfit = pl.pallas_call(
         functools.partial(kernel, cfg),
-        out_shape=(jax.ShapeDtypeStruct((local_p, local_w), f32),
-                   jax.ShapeDtypeStruct((local_p, local_w), f32),
+        out_shape=(jax.ShapeDtypeStruct((local_w, local_p), f32),
+                   jax.ShapeDtypeStruct((local_w, local_p), f32),
                    jax.ShapeDtypeStruct((1, comps, 2, bins), f32)),
         in_specs=[pl.BlockSpec(memory_space=pl.ANY),
-                  pl.BlockSpec(memory_space=pltpu.VMEM),
-                  pl.BlockSpec(memory_space=pltpu.VMEM),
+                  pl.BlockSpec(memory_space=pl.ANY),
+                  pl.BlockSpec(memory_space=pl.ANY),
                   pl.BlockSpec(memory_space=pltpu.SMEM)],
         out_specs=(pl.BlockSpec(memory_space=pltpu.VMEM),) * 3,
         scratch_shapes=[
             pltpu.VMEM((1, comps, 2, patches, bins), jnp.bfloat16),
             pltpu.VMEM((2 * comps, bins, patches), jnp.bfloat16),
             pltpu.SemaphoreType.DMA,
+            pltpu.VMEM((1, comps, 2, bins), f32),
+            pltpu.SemaphoreType.DMA,
+            pltpu.VMEM((local_w, local_p), jnp.int32),
+            pltpu.SemaphoreType.DMA,
             pltpu.VMEM((LANES, max(bins, patches)), f32),
-            pltpu.VMEM((1, local_w, LANES), f32),
+            pltpu.VMEM((local_w, LANES), f32),
             pltpu.VMEM((ndev, local_w, LANES), f32),
             pltpu.VMEM((windows, patches), jnp.int32),
             pltpu.VMEM((windows, 1, patches), jnp.int32),
@@ -358,17 +376,20 @@
             pltpu.VMEM((4 * npair, LANES, patches), f32),
             pltpu.VMEM((bins, LANES), f32),
             pltpu.VMEM((windows, patches), f32),
-            pltpu.VMEM((patches, LANES), f32),
-            pltpu.VMEM((ndev, 1, width + LANES), f32),
-            pltpu.VMEM((turns, ndev, 1, width + LANES), f32),
-            pltpu.VMEM((1, 1, width), f32),
-            pltpu.VMEM((turns, ndev, 1, width), f32),
-            pltpu.SemaphoreType.DMA((1 + 2 * turns,)),
-            pltpu.SemaphoreType.DMA((1 + 2 * turns,)),
+            pltpu.VMEM((patches + LANES, LANES), f32),
+            pltpu.VMEM((nsta, group_rows, width + LANES), f32),
+            pltpu.VMEM((turns, nsta, group_rows, width + LANES), f32),
+            pltpu.VMEM((group_rows, width + LANES), f32),
+            pltpu.VMEM((turns, nwin, group_rows, width + LANES), f32),
+            pltpu.VMEM((group_rows, width), f32),
+            pltpu.VMEM((turns, nsta, group_rows, width), f32),
+            pltpu.SemaphoreType.DMA((1 + 3 * turns,)),
+            pltpu.SemaphoreType.DMA((1 + 3 * turns,)),
         ],
         compiler_params=pltpu.CompilerParams(
             collective_id=0, has_side_effects=True, vmem_limit_bytes=56 * 2**20),
-    )(green, records, onsets, mask)
+    )(green, records, onsets.T, mask)
+    return slip.T, direction.T, misfit
 
 
 def solution(mesh):

time: 69.4 us -> 70.4 us (1.014)
  Pallas kernels: 62.8 us -> 65.5 us
  local copies, waits for them, and re-layouts: 5.42 us -> 3.84 us
    pallas_call x2 -> x0, local copies, waits for them, and re-layouts: 2.76 us -> none  [local(): pl.pallas_call(functools.partial(kernel, cfg), out_shape=(jax.ShapeDtypeS...]
    pallas_call x1, Pallas kernels: 62.8 us -> 65.5 us  [local(): pl.pallas_call(functools.partial(kernel, cfg), out_shape=(jax.ShapeDtypeS...]
    unnamed x2 -> x3, local copies, waits for them, and re-layouts: 2.67 us -> 3.84 us
where the time goes in v3:
time: 70.4 us; the launch traced here: 70 us
  Pallas kernels  65.5 us (93%)
  local copies, waits for them, and re-layouts  3.84 us (5%)
    pallas_call x1, Pallas kernels, local(): pl.pallas_call(functools.partial(kernel, cfg), out_shape=(jax.ShapeDtypeS...  65.5 us
    unnamed x3, local copies, waits for them, and re-layouts  3.84 us

profile of v3, /device:TPU:0, one launch (start us, length us, event | category | flops | bytes accessed | tf_op | source)
XLA Modules:
  0.0 70.0 jit_solution(16200190417726080564)
XLA Ops:
  0.6 65.5 %shard_map.67 = (f32[8,32]{1,0:T(8,128)}, f32[8,32]{1,0:T(8,128)}, f32[1,3,2,512]{3,2,1,0:T(2,128)}) custom-call(bf16[1,3,2,256,512]{4,3,2,1,0:T(8,128)(2,1)} %green_in.1, f32[1,3,2,512]{3,2,1,0:T(2,128)} %rec_in.1, s32[8,32]{1,0:T(8,128)} %bitcast.3, s32[1,3]{1,0:T(1,128)} %mask.1), custom_call_target="tpu_custom_call" | custom-call | tf_op jit(solution)/shard_map/pallas_call | solution.py:348
  66.2 1.3 %copy.10 = f32[32,8]{0,1:T(8,128)} copy(f32[32,8]{0,1:T(8,128)} %bitcast.5) | data formatting | bytes 2048
  67.4 1.3 %copy.11 = f32[32,8]{0,1:T(8,128)} copy(f32[32,8]{0,1:T(8,128)} %bitcast.4) | data formatting | bytes 2048
  68.7 1.3 %copy.12 = f32[1,3,2,512]{3,2,1,0:T(2,128)} copy(f32[1,3,2,512]{3,2,1,0:T(2,128)} %get-tuple-element.14) | data formatting | bytes 24576
